TPU v7x, 32 devices: a whole 2x2x4 slice. The times are simulated.
32 devices in a mesh: layer: 32 (over z, y, x, core).
Axes of the slice: x: 2, y: 2, z: 4, core: 2. Of those that a mesh axis runs over, the one named last changes fastest.
Arguments:
- lower_block: float32 [32, 512, 512], P('layer'), may hold values from -0.109375 to 0.109375
- upper_block: float32 [32, 512, 512], P('layer'), may hold values from -0.109375 to 0.109375
- right_side: float32 [32, 64, 512], P('layer'), may hold values from -6 to 6
Outputs:
- reduced_lower: float32 [32, 512, 512], P('layer')
- reduced_upper: float32 [32, 512, 512], P('layer')
- reduced_rhs: float32 [32, 64, 512], P('layer')
All inputs are finite; a program needn't handle non-finite values.
Results may differ from a plain program's by a relative error of at most 0.00022.
Values sent between devices are 32-bit elements; how exact they have to be, the bound alone decides.
A program may use at most 64 MiB of HBM per device.

v0:
```python
import math

import jax
import jax.numpy as jnp
from jax import lax
from jax.sharding import PartitionSpec as P

BLOCK = 512
LEVELS = 3
CHAINS = 8


def from_behind(value, axis, by):
    peers = lax.axis_size(axis)
    return lax.ppermute(value, axis, [(i, (i + by) % peers) for i in range(peers)])


def matmul_high(left, right):
    return jnp.dot(left, right, precision=lax.Precision.HIGHEST, preferred_element_type=jnp.float32)


def rows_times(block, columns):
    return lax.dot_general(
        columns,
        block,
        (((1,), (1,)), ((), ())),
        precision=lax.Precision.HIGHEST,
        preferred_element_type=jnp.float32,
    )


def reduce_level(own, from_below, from_above):
    order_size = BLOCK
    own_lower = own[:order_size]
    own_upper = own[order_size : 2 * order_size]
    own_rhs = own[2 * order_size :]
    identity = jnp.eye(order_size, dtype=jnp.float32)
    diagonal = (
        identity
        - matmul_high(own_lower, from_below[order_size : 2 * order_size])
        - matmul_high(own_upper, from_above[:order_size])
    )
    initial = 2.0 * identity - diagonal
    inverse = matmul_high(initial, 2.0 * identity - matmul_high(diagonal, initial))
    new_lower = -matmul_high(inverse, matmul_high(own_lower, from_below[:order_size]))
    new_upper = -matmul_high(
        inverse, matmul_high(own_upper, from_above[order_size : 2 * order_size])
    )
    new_rhs = (
        own_rhs
        - rows_times(own_lower, from_below[2 * order_size :])
        - rows_times(own_upper, from_above[2 * order_size :])
    )
    new_rhs = rows_times(inverse, new_rhs)
    return jnp.concatenate([new_lower, new_upper, new_rhs], axis=0)


def per_device(lower_block, upper_block, right_side):
    payload = jnp.concatenate([lower_block[0], upper_block[0], right_side[0]], axis=0)
    for level_index in range(LEVELS):
        stride = 2**level_index
        from_below = from_behind(payload, "layer", stride)
        from_above = from_behind(payload, "layer", -stride)
        payload = reduce_level(payload, from_below, from_above)
    device_count = lax.axis_size("layer")
    flat_pieces = payload.reshape(device_count, -1)
    spread_pieces = lax.all_to_all(flat_pieces, "layer", split_axis=0, concat_axis=0, tiled=True)
    chain_len = device_count // CHAINS
    spread_pieces = jnp.transpose(spread_pieces.reshape(chain_len, CHAINS, -1), (1, 0, 2)).reshape(
        device_count, -1
    )
    flat_pieces = lax.all_to_all(spread_pieces, "layer", split_axis=0, concat_axis=0, tiled=True)
    payload = flat_pieces.reshape(payload.shape)
    factor = 2.5**8 * math.sqrt(BLOCK)
    reduced_lower = payload[:BLOCK] * factor
    reduced_upper = payload[BLOCK : 2 * BLOCK] * factor
    reduced_rhs = payload[2 * BLOCK :]
    return (reduced_lower[None], reduced_upper[None], reduced_rhs[None])


def solution(mesh):
    placed = (P("layer", None, None), P("layer", None, None), P("layer", None, None))
    return jax.shard_map(
        per_device,
        mesh=mesh,
        in_specs=placed,
        out_specs=(P("layer", None, None), P("layer", None, None), P("layer", None, None)),
        check_vma=False,
    )
```

profile of v0, /device:TPU:2, one launch (start us, length us, event | category | flops | bytes accessed | tf_op | source)
XLA Modules:
  0.0 460.3 jit_solution(11345765337344938649)
XLA Ops:
  0.6 1.9 pad_maximum_fusion
  3.1 46.5 %collective-permute-done.1 = f32[1088,512]{1,0:T(8,128)S(1)} collective-permute-done((f32[1088,512]{1,0:T(8,128)S(1)}, f32[1088,512]{1,0:T(8,128)S(1)}, u32[]{:S(2)}, u32[]{:S(2)}) %collective-permute-start.1) | collective-permute-done | bytes 2228256 | tf_op jit(solution)/shard_map/ppermute | solution.py:15
  49.6 3.5 convolution_bitcast_fusion
  53.4 3.5 fusion
  56.9 1.9 select_subtract_fusion.4
  58.8 3.5 fusion.3
  65.9 3.5 fusion.25
  69.4 1.9 convolution_negate_fusion.5
  71.3 3.5 fusion.23
  74.7 11.4 %convolution_negate_fusion.4 = f32[512,512]{1,0:T(8,128)S(1)} fusion(f32[512,512]{1,0:T(8,128)S(1)} %fusion.3, f32[512,512]{1,0:T(8,128)S(1)} %fusion.23), kind=kOutput, calls=%fused_computation.18 | convolution fusion | flops 1610874880 | bytes 3145728 | tf_op jit(solution)/shard_map/dot_general | solution.py:19
  86.4 3.9 collective-permute-start.2
  90.2 47.0 %collective-permute-done.3 = f32[1088,512]{1,0:T(8,128)S(1)} collective-permute-done((f32[1088,512]{1,0:T(8,128)S(1)}, f32[1088,512]{1,0:T(8,128)S(1)}, u32[]{:S(2)}, u32[]{:S(2)}) %collective-permute-start.3) | collective-permute-done | bytes 2228256 | tf_op jit(solution)/shard_map/ppermute | solution.py:15
  137.2 1.9 fusion.20
  139.1 46.7 %collective-permute-done.2 = f32[1088,512]{1,0:T(8,128)S(1)} collective-permute-done((f32[1088,512]{1,0:T(8,128)S(1)}, f32[1088,512]{1,0:T(8,128)S(1)}, u32[]{:S(2)}, u32[]{:S(2)}) %collective-permute-start.2) | collective-permute-done | bytes 2228256 | tf_op jit(solution)/shard_map/ppermute | solution.py:15
  185.8 1.9 fusion.1
  187.7 1.9 select_subtract_fusion.2
  189.6 3.5 fusion.4
  196.5 2.1 fusion.18
  200.4 1.9 fusion.16
  204.3 6.2 %collective-permute-start.5 = (f32[1088,512]{1,0:T(8,128)S(1)}, f32[1088,512]{1,0:T(8,128)S(1)}, u32[]{:S(2)}, u32[]{:S(2)}) collective-permute-start(f32[1088,512]{1,0:T(8,128)S(1)} %pad_maximum_fusion.2), channel_id=1, source_target_pairs={{0,28},{1,29},{2,30},{3,31},{4,0},{5,1},{6,2},{7,3},{8,4},{9,5},{1... | collective-permute-start | bytes 6684680 | tf_op jit(solution)/shard_map/ppermute | solution.py:15
  211.0 93.3 %collective-permute-done.5 = f32[1088,512]{1,0:T(8,128)S(1)} collective-permute-done((f32[1088,512]{1,0:T(8,128)S(1)}, f32[1088,512]{1,0:T(8,128)S(1)}, u32[]{:S(2)}, u32[]{:S(2)}) %collective-permute-start.5) | collective-permute-done | bytes 2228256 | tf_op jit(solution)/shard_map/ppermute | solution.py:15
  304.3 1.9 fusion.13
  306.2 1.9 fusion.2
  308.1 1.9 select_subtract_fusion
  310.0 3.5 fusion.5
  316.8 2.0 fusion.9
  320.7 1.9 fusion.11
  324.7 3.7 all_to_all.16
  328.4 58.4 %all_to_all.19 = f32[32,1,17408]{2,1,0:T(1,128)S(1)} all-to-all(f32[32,1,17408]{2,1,0:T(1,128)} %all_to_all.16), channel_id=1, replica_groups=mesh['layer'=32] {'layer'}, dimensions={0} | all-to-all | bytes 4456448 | tf_op jit(solution)/shard_map/all_to_all | solution.py:67
  388.6 4.1 all_to_all.14
  392.7 56.1 %all_to_all.20 = f32[32,1,17408]{2,1,0:T(1,128)S(1)} all-to-all(f32[32,1,17408]{2,1,0:T(1,128)} %all_to_all.14), channel_id=1, replica_groups=mesh['layer'=32] {'layer'}, dimensions={0} | all-to-all | bytes 4456448 | tf_op jit(solution)/shard_map/all_to_all | solution.py:72
  448.8 7.3 %reduce = f32[32,17408]{1,0:T(8,128)} reduce(f32[32,1,17408]{2,1,0:T(1,128)S(1)} %all_to_all.20, f32[]{:T(128)} %constant.9), dimensions={1}, to_apply=%all_to_all.15.reduce_sub_computation | reduce | bytes 4456452 | tf_op jit(solution)/shard_map/all_to_all | solution.py:72
  (33 shorter events, 25.5 us)
Async XLA Ops:
  0.6 49.0 %copy-start = (f32[1,512,512]{2,1,0:T(8,128)S(1)}, f32[1,512,512]{2,1,0:T(8,128)}, u32[]{:S(2)}) copy-start(f32[1,512,512]{2,1,0:T(8,128)} %param.4) | copy-start | bytes 3145732
  2.5 50.9 %copy-start.1 = (f32[1,512,512]{2,1,0:T(8,128)S(1)}, f32[1,512,512]{2,1,0:T(8,128)}, u32[]{:S(2)}) copy-start(f32[1,512,512]{2,1,0:T(8,128)} %param.3) | copy-start | bytes 3145732
  2.5 47.1 %collective-permute-start.1 = (f32[1088,512]{1,0:T(8,128)S(1)}, f32[1088,512]{1,0:T(8,128)S(1)}, u32[]{:S(2)}, u32[]{:S(2)}) collective-permute-start(f32[1088,512]{1,0:T(8,128)S(1)} %pad_maximum_fusion), channel_id=1, source_target_pairs={{0,31},{1,0},{2,1},{3,2},{4,3},{5,4},{6,5},{7,6},{8,7},{9,8},{10,9... | collective-permute-start | bytes 6684680 | tf_op jit(solution)/shard_map/ppermute | solution.py:15
  2.6 50.8 %collective-permute-start = (f32[1088,512]{1,0:T(8,128)S(1)}, f32[1088,512]{1,0:T(8,128)S(1)}, u32[]{:S(2)}, u32[]{:S(2)}) collective-permute-start(f32[1088,512]{1,0:T(8,128)S(1)} %pad_maximum_fusion), channel_id=1, source_target_pairs={{0,1},{1,2},{2,3},{3,4},{4,5},{5,6},{6,7},{7,8},{8,9},{9,10},{10,1... | collective-permute-start | bytes 6684680 | tf_op jit(solution)/shard_map/ppermute | solution.py:15
  58.8 4.9 %copy-start.2 = (f32[1,64,512]{2,1,0:T(8,128)S(1)}, f32[1,64,512]{2,1,0:T(8,128)}, u32[]{:S(2)}) copy-start(f32[1,64,512]{2,1,0:T(8,128)} %param.5) | copy-start | bytes 393220
  86.3 50.9 %collective-permute-start.3 = (f32[1088,512]{1,0:T(8,128)S(1)}, f32[1088,512]{1,0:T(8,128)S(1)}, u32[]{:S(2)}, u32[]{:S(2)}) collective-permute-start(f32[1088,512]{1,0:T(8,128)S(1)} %pad_maximum_fusion.1), channel_id=1, source_target_pairs={{0,30},{1,31},{2,0},{3,1},{4,2},{5,3},{6,4},{7,5},{8,6},{9,7},{10,... | collective-permute-start | bytes 6684680 | tf_op jit(solution)/shard_map/ppermute | solution.py:15
  86.4 99.4 %collective-permute-start.2 = (f32[1088,512]{1,0:T(8,128)S(1)}, f32[1088,512]{1,0:T(8,128)S(1)}, u32[]{:S(2)}, u32[]{:S(2)}) collective-permute-start(f32[1088,512]{1,0:T(8,128)S(1)} %pad_maximum_fusion.1), channel_id=1, source_target_pairs={{0,2},{1,3},{2,4},{3,5},{4,6},{5,7},{6,8},{7,9},{8,10},{9,11},{10,... | collective-permute-start | bytes 6684680 | tf_op jit(solution)/shard_map/ppermute | solution.py:15
  204.3 99.9 %collective-permute-start.5 = (f32[1088,512]{1,0:T(8,128)S(1)}, f32[1088,512]{1,0:T(8,128)S(1)}, u32[]{:S(2)}, u32[]{:S(2)}) collective-permute-start(f32[1088,512]{1,0:T(8,128)S(1)} %pad_maximum_fusion.2), channel_id=1, source_target_pairs={{0,28},{1,29},{2,30},{3,31},{4,0},{5,1},{6,2},{7,3},{8,4},{9,5},{1... | collective-permute-start | bytes 6684680 | tf_op jit(solution)/shard_map/ppermute | solution.py:15
  210.6 95.6 %collective-permute-start.4 = (f32[1088,512]{1,0:T(8,128)S(1)}, f32[1088,512]{1,0:T(8,128)S(1)}, u32[]{:S(2)}, u32[]{:S(2)}) collective-permute-start(f32[1088,512]{1,0:T(8,128)S(1)} %pad_maximum_fusion.2), channel_id=1, source_target_pairs={{0,4},{1,5},{2,6},{3,7},{4,8},{5,9},{6,10},{7,11},{8,12},{9,13},{1... | collective-permute-start | bytes 6684680 | tf_op jit(solution)/shard_map/ppermute | solution.py:15
where the time goes:
time: 467 us; the launch traced here: 460 us
  waiting for transfers between devices  234 us (50%)
  blocking collectives  114 us (24%)
  matrix products  76.4 us (16%)
  local copies, waits for them, and re-layouts  12.1 us (3%)
  other arithmetic  11.3 us (2%)
  starting transfers between devices  11.1 us (2%)
    ppermute x6, waiting for transfers between devices, from_behind(): lax.ppermute(value, axis, [(i, (i + by) % peers) for i in range(peers)])  234 us
    dot_general x24, matrix products, matmul_high(): jnp.dot(left, right, precision=lax.Precision.HIGHEST, preferred_element_t...  66.1 us
    all_to_all x1, blocking collectives, per_device(): lax.all_to_all(flat_pieces, 'layer', split_axis=0, concat_axis=0, tiled=T...  58.4 us
    all_to_all x1, blocking collectives, per_device(): lax.all_to_all(spread_pieces, 'layer', split_axis=0, concat_axis=0, tiled...  56.1 us
    ppermute x6, starting transfers between devices, from_behind(): lax.ppermute(value, axis, [(i, (i + by) % peers) for i in range(peers)])  11.1 us
    dot_general x9, matrix products, rows_times(): lax.dot_general(columns, block, (((1,), (1,)), ((), ())), precision=lax.P...  10.4 us
  transfers between devices with their start and end apart: 6, of which 5 were waited for; matrix products, arithmetic and copies ran while one was open for 2% of the time, Pallas kernels for 0%

commit v1 on v0

v1 whole, which is shorter than its diff:
```python
import functools
import math

import jax
import jax.numpy as jnp
from jax import lax
from jax.experimental import pallas as pl
from jax.experimental.pallas import tpu as pltpu
from jax.sharding import PartitionSpec as P

LEVELS = 3
CHAINS = 8
F32, BF16 = jnp.float32, jnp.bfloat16
MESH = pl.DeviceIdType.MESH


def halves(value):
    high = value.astype(BF16)
    return high, (value - high.astype(F32)).astype(BF16)


def dot3(a_high, a_low, b_high, b_low, transposed=False):
    dims = (((1,), (1 if transposed else 0,)), ((), ()))
    dot = lambda a, b: lax.dot_general(a, b, dims, preferred_element_type=F32)
    return dot(a_high, b_high) + (dot(a_high, b_low) + dot(a_low, b_high))


def kernel(n, order, columns, factor, lower_ref, upper_ref, rhs_ref, out_lower, out_upper, out_rhs,
           bufs, fin, term, sh, sl, nh, nl, fh, fl, eh, el, qh, ql, yh, yl, xh, xl,
           load_sem, send_sem, recv_sem, fin_send, fin_recv):
    me = lax.axis_index("layer")
    half = order // 2
    chain_len = n // CHAINS
    core = me % 2
    mate = me + 1 - 2 * core
    f = core
    far_step = lambda step, sign: (me + sign * step + n) % n

    def other_core(dev):
        return dev + 1 - 2 * (dev % 2)

    roles = []
    for level in range(2):
        bit = 2 << level
        side = (me // bit) % 2
        across = me + bit * (1 - 2 * side)
        sign = 1 - 2 * side
        roles.append((
            side == core,
            across,
            other_core(across),
            other_core(far_step(2 * bit, sign)),
            other_core(far_step(2 * bit, -sign)),
        ))
    last_far = other_core(far_step(CHAINS, 2 * core - 1))
    chain = 4 * core + 2 * ((me // 4) % 2) + (me // 2) % 2
    goes_to = chain * chain_len + me // CHAINS
    my_chain, my_place = me // chain_len, me % chain_len
    comes_from = CHAINS * my_place + 4 * ((my_chain // 2) % 2) + 2 * (my_chain % 2) + my_chain // 4
    moves = goes_to != me

    def rows_of(piece, first):
        which = (piece // 2 + first) % 2
        return pl.ds(pl.multiple_of(which * order + (piece % 2) * half, half), half)

    def tail_rows():
        return pl.ds(2 * order, columns)

    def remote(level, from_slot, to_slot, flow, piece, rows, dev):
        return pltpu.make_async_remote_copy(
            src_ref=bufs.at[level, from_slot, rows],
            dst_ref=bufs.at[level, to_slot, rows],
            send_sem=send_sem.at[level, flow, piece],
            recv_sem=recv_sem.at[level, to_slot - 1, piece],
            device_id=(dev,),
            device_id_type=MESH,
        )

    def flows(level):
        if level < 2:
            outer, across, diagonal, relay, _ = roles[level]
            return ((outer, 2, 0, across), (jnp.logical_not(outer), 1, 0, diagonal), (jnp.logical_not(outer), 1, 1, mate))
        always = core >= 0
        return ((always, 2, 0, last_far), (always, 1, 1, mate))

    def piece_rows(piece, first):
        return tail_rows() if isinstance(piece, int) and piece == 4 else rows_of(piece, first)

    def send_own(level, piece):
        for when, slot, flow, dev in flows(level):
            @pl.when(when)
            def _():
                remote(level, 0, slot, flow, piece, piece_rows(piece, f), dev).start()

    barrier = pltpu.get_barrier_semaphore()

    def greet(dev):
        pl.semaphore_signal(barrier, inc=1, device_id=(dev,), device_id_type=MESH)

    loads = []
    for index, (ref, start, size) in enumerate(((upper_ref, 0, order), (lower_ref, order, order), (rhs_ref, 2 * order, columns))):
        copy = pltpu.make_async_copy(ref.at[0], bufs.at[0, 0, pl.ds(start, size)], load_sem.at[index])
        copy.start()
        loads.append(copy)

    for level in range(2):
        outer, across, diagonal, relay, relayed_by = roles[level]

        @pl.when(outer)
        def _():
            greet(mate)
            greet(relayed_by)

        @pl.when(jnp.logical_not(outer))
        def _():
            greet(diagonal)
            greet(across)

    greet(mate)
    greet(last_far)

    @pl.when(moves)
    def _():
        greet(comes_from)

    expected = 2 + moves.astype(jnp.int32)
    for level in range(2):
        expected += jnp.where(roles[level][0], 1, 3)
    pl.semaphore_wait(barrier, expected)

    for copy in loads:
        copy.wait()
    for piece in range(5):
        send_own(0, piece)

    def block(r):
        return pl.ds(pl.multiple_of(r * half, half), half)

    def split_into(level, slot, which, high_ref, low_ref):
        @pl.loop(0, 2)
        def _(r):
            rows = pl.ds(pl.multiple_of(which * order + r * half, half), half)
            high, low = halves(bufs[level, slot, rows, :])
            high_ref[which, block(r), :] = high
            low_ref[which, block(r), :] = low

    def multiply(a_high, a_low, b_high, b_low, done):
        @pl.loop(0, 2)
        def _(r):
            done(r, dot3(a_high[block(r), :], a_low[block(r), :], b_high[...], b_low[...]))

    def store_split(high_ref, low_ref):
        def done(r, value):
            high, low = halves(value)
            high_ref[block(r), :] = high
            low_ref[block(r), :] = low
        return done

    for level in range(LEVELS):
        if level < 2:
            outer, across, diagonal, relay, _ = roles[level]
            inner = jnp.logical_not(outer)
            self_slot = jnp.where(outer, 0, 1)
            first = jnp.where(outer, 1 - f, f)
        else:
            outer, inner, relay = core >= 0, None, None
            self_slot = 0
            first = 1 - f
        near_slot = 1 - self_slot

        def wait_slot(slot, piece, rows):
            remote(level, 0, slot, 0, piece, rows, mate).wait_recv()

        def take_far(piece):
            wait_slot(2, piece, piece_rows(piece, first))

        if inner is not None:
            @pl.when(inner)
            def _():
                for piece in range(5):
                    take_far(piece)
                    remote(level, 2, 2, 2, piece, piece_rows(piece, first), relay).start()

        for piece in range(5):
            wait_slot(1, piece, piece_rows(piece, 1 - f))

        for which in range(2):
            split_into(level, self_slot, which, sh, sl)
            split_into(level, near_slot, which, nh, nl)

        def add_term(r, value):
            term[block(r), :] = value

        multiply(sh.at[f], sl.at[f], nh.at[1 - f], nl.at[1 - f], add_term)
        multiply(sh.at[f], sl.at[f], nh.at[f], nl.at[f], store_split(xh.at[f], xl.at[f]))

        @pl.when(outer)
        def _():
            for piece in range(5):
                take_far(piece)

        split_into(level, 2, 0, fh, fl)
        split_into(level, 2, 1, fh, fl)

        def finish_e(r, value):
            high, low = halves(term[block(r), :] + value)
            eh[block(r), :] = high
            el[block(r), :] = low

        multiply(sh.at[1 - f], sl.at[1 - f], fh.at[f], fl.at[f], finish_e)
        multiply(eh, el, eh, el, store_split(qh, ql))

        def finish_y(r, value):
            rows = lax.broadcasted_iota(jnp.int32, (half, order), 0) + r * half
            cols = lax.broadcasted_iota(jnp.int32, (half, order), 1)
            eye = jnp.where(rows == cols, 1.0, 0.0).astype(F32)
            e = eh[block(r), :].astype(F32) + el[block(r), :].astype(F32)
            q = qh[block(r), :].astype(F32) + ql[block(r), :].astype(F32)
            high, low = halves(eye + (e + (q + value)))
            yh[block(r), :] = high
            yl[block(r), :] = low

        multiply(eh, el, qh, ql, finish_y)

        def emit(piece):
            which = (piece // 2 + f) % 2
            r = piece % 2
            value = dot3(yh[block(r), :], yl[block(r), :], xh[which], xl[which])
            rows = rows_of(piece, f)
            if level < LEVELS - 1:
                bufs[level + 1, 0, rows, :] = -value
                send_own(level + 1, piece)
            else:
                fin[rows, :] = value * (-factor)
                send_fin(piece, which, r)

        def fin_copy(piece, out, out_rows, rows):
            return pltpu.make_async_remote_copy(
                src_ref=fin.at[rows], dst_ref=out.at[0, out_rows],
                send_sem=fin_send.at[piece], recv_sem=fin_recv.at[piece],
                device_id=(goes_to,), device_id_type=MESH)

        def fin_local(piece, out, out_rows, rows):
            return pltpu.make_async_copy(fin.at[rows], out.at[0, out_rows], load_sem.at[piece])

        def send_fin_to(out, key, out_rows, rows):
            @pl.when(moves)
            def _():
                fin_copy(key, out, out_rows, rows).start()

            @pl.when(jnp.logical_not(moves))
            def _():
                fin_local(key, out, out_rows, rows).start()

        def send_fin(piece, which, r):
            rows = rows_of(piece, f)

            @pl.when(which == 0)
            def _():
                send_fin_to(out_upper, r, block(r), rows)

            @pl.when(which == 1)
            def _():
                send_fin_to(out_lower, 2 + r, block(r), rows)

        @pl.loop(0, 2)
        def _(piece):
            emit(piece)

        multiply(sh.at[1 - f], sl.at[1 - f], fh.at[1 - f], fl.at[1 - f], store_split(xh.at[1 - f], xl.at[1 - f]))

        @pl.loop(2, 4)
        def _(piece):
            emit(piece)

        near_high, near_low = halves(bufs[level, near_slot, tail_rows(), :])
        far_high, far_low = halves(bufs[level, 2, tail_rows(), :])
        right = (bufs[level, self_slot, tail_rows(), :]
                 - dot3(near_high, near_low, sh[f], sl[f], True)
                 - dot3(far_high, far_low, sh[1 - f], sl[1 - f], True))
        right_high, right_low = halves(right)
        right = dot3(right_high, right_low, yh[...], yl[...], True)
        if level < LEVELS - 1:
            bufs[level + 1, 0, tail_rows(), :] = right
            send_own(level + 1, 4)
        else:
            fin[tail_rows(), :] = right
            send_fin_to(out_rhs, 4, pl.ds(0, columns), tail_rows())

    for level in range(LEVELS):
        for when, slot, flow, dev in flows(level):
            @pl.when(when)
            def _():
                for piece in range(5):
                    remote(level, 0, slot, flow, piece, piece_rows(piece, f), dev).wait_send()
        if level < 2:
            outer, across, diagonal, relay, _ = roles[level]

            @pl.when(jnp.logical_not(outer))
            def _():
                for piece in range(5):
                    remote(level, 2, 2, 2, piece, piece_rows(piece, f), relay).wait_send()

    ends = [(r + 2 * w, out, pl.ds(r * half, half), pl.ds(w * order + r * half, half))
            for w, out in ((0, out_upper), (1, out_lower)) for r in range(2)]
    ends.append((4, out_rhs, pl.ds(0, columns), tail_rows()))
    for key, out, out_rows, rows in ends:
        @pl.when(moves)
        def _():
            copy = fin_copy(key, out, out_rows, rows)
            copy.wait_send()
            copy.wait_recv()

        @pl.when(jnp.logical_not(moves))
        def _():
            fin_local(key, out, out_rows, rows).wait()


def per_device(lower_block, upper_block, right_side):
    n = lax.axis_size("layer")
    order, columns = lower_block.shape[2], right_side.shape[1]
    rows = 2 * order + columns
    pair = lambda: pltpu.VMEM((2, order, order), BF16)
    one = lambda: pltpu.VMEM((order, order), BF16)
    return pl.pallas_call(
        functools.partial(kernel, n, order, columns, 2.5**8 * math.sqrt(order)),
        out_shape=[jax.ShapeDtypeStruct(a.shape, F32) for a in (lower_block, upper_block, right_side)],
        in_specs=[pl.BlockSpec(memory_space=pl.ANY)] * 3,
        out_specs=[pl.BlockSpec(memory_space=pltpu.VMEM)] * 3,
        scratch_shapes=[
            pltpu.VMEM((LEVELS, 3, rows, order), F32),
            pltpu.VMEM((rows, order), F32),
            pltpu.VMEM((order, order), F32),
            pair(), pair(), pair(), pair(), pair(), pair(),
            one(), one(), one(), one(), one(), one(),
            pair(), pair(),
            pltpu.SemaphoreType.DMA((5,)),
            pltpu.SemaphoreType.DMA((LEVELS, 3, 5)),
            pltpu.SemaphoreType.DMA((LEVELS, 2, 5)),
            pltpu.SemaphoreType.DMA((5,)),
            pltpu.SemaphoreType.DMA((5,)),
        ],
        compiler_params=pltpu.CompilerParams(
            collective_id=0, has_side_effects=True, vmem_limit_bytes=60 * 1024 * 1024
        ),
    )(lower_block, upper_block, right_side)


def solution(mesh):
    placed = (P("layer", None, None), P("layer", None, None), P("layer", None, None))
    return jax.shard_map(
        per_device,
        mesh=mesh,
        in_specs=placed,
        out_specs=placed,
        check_vma=False,
    )
```

time: 467 us -> 253 us (0.54)
  the two profiles are of different devices: /device:TPU:2 before, /device:TPU:1 now
where the time goes in v1:
time: 253 us
  Pallas kernels  248 us (98%)
  local copies, waits for them, and re-layouts  4.03 us (2%)
    pallas_call x1, Pallas kernels, per_device(): pl.pallas_call(functools.partial(kernel, n, order, columns, 2.5 ** 8 * ma...  248 us

profile of v1, /device:TPU:1, one launch (start us, length us, event | category | flops | bytes accessed | tf_op | source)
XLA Modules:
  0.0 252.8 jit_solution(5827989854671948184)
XLA Ops:
  0.6 248.2 %shard_map.58 = (f32[1,512,512]{2,1,0:T(8,128)}, f32[1,512,512]{2,1,0:T(8,128)}, f32[1,64,512]{2,1,0:T(8,128)}) custom-call(f32[1,512,512]{2,1,0:T(8,128)} %lower_ref.1, f32[1,512,512]{2,1,0:T(8,128)} %upper_ref.1, f32[1,64,512]{2,1,0:T(8,128)} %rhs_ref.1), custom_call_target="tpu_custom_call" | custom-call | tf_op jit(solution)/shard_map/pallas_call | solution.py:325
  248.8 0.0 copy-start
  248.8 2.4 copy.9
  251.2 0.0 copy-done
  251.2 0.0 copy-start.1
  251.2 1.0 copy.10
  252.1 0.1 copy-done.1
  252.2 0.7 copy.11
Async XLA Ops:
  248.8 2.4 copy-start
  251.2 1.0 copy-start.1

commit v2 on v1

--- a/solution.py
+++ b/solution.py
@@ -27,7 +27,7 @@
 
 def kernel(n, order, columns, factor, lower_ref, upper_ref, rhs_ref, out_lower, out_upper, out_rhs,
            bufs, fin, term, sh, sl, nh, nl, fh, fl, eh, el, qh, ql, yh, yl, xh, xl,
-           load_sem, send_sem, recv_sem, fin_send, fin_recv):
+           load_sem, send_sem, recv_sem, fin_send, fin_recv, passing, pass_send, pass_recv):
     me = lax.axis_index("layer")
     half = order // 2
     chain_len = n // CHAINS
@@ -58,6 +58,25 @@
     my_chain, my_place = me // chain_len, me % chain_len
     comes_from = CHAINS * my_place + 4 * ((my_chain // 2) % 2) + 2 * (my_chain % 2) + my_chain // 4
     moves = goes_to != me
+    groups = n // CHAINS
+
+    def detour(dev):
+        group, side, at_core = dev // CHAINS, (dev // 4) % 2, dev % 2
+        low = (group == 1) & (side == 0) & (at_core == 0)
+        high = (group == groups - 2) & (side == 1) & (at_core == 1)
+        return low | high
+
+    def y_partner(dev):
+        return dev + 4 * (1 - 2 * ((dev // 4) % 2))
+
+    def home(dev):
+        return (4 * (dev % 2) + 2 * ((dev // 4) % 2) + (dev // 2) % 2) * chain_len + dev // CHAINS
+
+    helped = y_partner(me)
+    helps = detour(helped)
+    detours = detour(me)
+    helped_home = home(helped)
+    greets = jnp.where(detour(comes_from), y_partner(comes_from), comes_from)
 
     def rows_of(piece, first):
         which = (piece // 2 + first) % 2
@@ -87,10 +106,17 @@
         return tail_rows() if isinstance(piece, int) and piece == 4 else rows_of(piece, first)
 
     def send_own(level, piece):
-        for when, slot, flow, dev in flows(level):
+        for at, (when, slot, flow, dev) in enumerate(flows(level)):
+            if level < 2 and at == 1:
+                continue
+
             @pl.when(when)
             def _():
                 remote(level, 0, slot, flow, piece, piece_rows(piece, f), dev).start()
+
+    def send_held(level, piece):
+        _, slot, flow, dev = flows(level)[1]
+        remote(level, 0, slot, flow, piece, piece_rows(piece, f), dev).start()
 
     barrier = pltpu.get_barrier_semaphore()
 
@@ -121,9 +147,13 @@
 
     @pl.when(moves)
     def _():
-        greet(comes_from)
-
-    expected = 2 + moves.astype(jnp.int32)
+        greet(greets)
+
+    @pl.when(helps)
+    def _():
+        greet(helped)
+
+    expected = 2 + moves.astype(jnp.int32) + helps.astype(jnp.int32)
     for level in range(2):
         expected += jnp.where(roles[level][0], 1, 3)
     pl.semaphore_wait(barrier, expected)
@@ -155,6 +185,40 @@
             high_ref[block(r), :] = high
             low_ref[block(r), :] = low
         return done
+
+    def fin_copy(key, out, out_rows, rows):
+        return pltpu.make_async_remote_copy(
+            src_ref=fin.at[rows], dst_ref=out.at[0, out_rows],
+            send_sem=fin_send.at[key], recv_sem=fin_recv.at[key],
+            device_id=(goes_to,), device_id_type=MESH)
+
+    def detour_copy(key, rows):
+        return pltpu.make_async_remote_copy(
+            src_ref=fin.at[rows], dst_ref=passing.at[rows],
+            send_sem=fin_send.at[key], recv_sem=pass_recv.at[key],
+            device_id=(helped,), device_id_type=MESH)
+
+    def pass_copy(key, out, out_rows, rows):
+        return pltpu.make_async_remote_copy(
+            src_ref=passing.at[rows], dst_ref=out.at[0, out_rows],
+            send_sem=pass_send.at[key], recv_sem=fin_recv.at[key],
+            device_id=(helped_home,), device_id_type=MESH)
+
+    def fin_local(key, out, out_rows, rows):
+        return pltpu.make_async_copy(fin.at[rows], out.at[0, out_rows], load_sem.at[key])
+
+    def send_fin_to(out, key, out_rows, rows):
+        @pl.when(moves & jnp.logical_not(detours))
+        def _():
+            fin_copy(key, out, out_rows, rows).start()
+
+        @pl.when(detours)
+        def _():
+            detour_copy(key, rows).start()
+
+        @pl.when(jnp.logical_not(moves))
+        def _():
+            fin_local(key, out, out_rows, rows).start()
 
     for level in range(LEVELS):
         if level < 2:
@@ -180,6 +244,9 @@
                 for piece in range(5):
                     take_far(piece)
                     remote(level, 2, 2, 2, piece, piece_rows(piece, first), relay).start()
+                    if piece >= 1:
+                        send_held(level, piece - 1)
+                send_held(level, 4)
 
         for piece in range(5):
             wait_slot(1, piece, piece_rows(piece, 1 - f))
@@ -233,24 +300,6 @@
             else:
                 fin[rows, :] = value * (-factor)
                 send_fin(piece, which, r)
-
-        def fin_copy(piece, out, out_rows, rows):
-            return pltpu.make_async_remote_copy(
-                src_ref=fin.at[rows], dst_ref=out.at[0, out_rows],
-                send_sem=fin_send.at[piece], recv_sem=fin_recv.at[piece],
-                device_id=(goes_to,), device_id_type=MESH)
-
-        def fin_local(piece, out, out_rows, rows):
-            return pltpu.make_async_copy(fin.at[rows], out.at[0, out_rows], load_sem.at[piece])
-
-        def send_fin_to(out, key, out_rows, rows):
-            @pl.when(moves)
-            def _():
-                fin_copy(key, out, out_rows, rows).start()
-
-            @pl.when(jnp.logical_not(moves))
-            def _():
-                fin_local(key, out, out_rows, rows).start()
 
         def send_fin(piece, which, r):
             rows = rows_of(piece, f)
@@ -287,6 +336,17 @@
             fin[tail_rows(), :] = right
             send_fin_to(out_rhs, 4, pl.ds(0, columns), tail_rows())
 
+    ends = [(r + 2 * w, out, pl.ds(r * half, half), pl.ds(w * order + r * half, half))
+            for w, out in ((0, out_upper), (1, out_lower)) for r in range(2)]
+    ends.append((4, out_rhs, pl.ds(0, columns), tail_rows()))
+
+    for at_core, turn in ((0, 0), (1, 2)):
+        @pl.when(helps & (core == at_core))
+        def _():
+            for key, out, out_rows, rows in ends[turn:4] + ends[:turn] + ends[4:]:
+                detour_copy(key, rows).wait_recv()
+                pass_copy(key, out, out_rows, rows).start()
+
     for level in range(LEVELS):
         for when, slot, flow, dev in flows(level):
             @pl.when(when)
@@ -301,15 +361,16 @@
                 for piece in range(5):
                     remote(level, 2, 2, 2, piece, piece_rows(piece, f), relay).wait_send()
 
-    ends = [(r + 2 * w, out, pl.ds(r * half, half), pl.ds(w * order + r * half, half))
-            for w, out in ((0, out_upper), (1, out_lower)) for r in range(2)]
-    ends.append((4, out_rhs, pl.ds(0, columns), tail_rows()))
     for key, out, out_rows, rows in ends:
         @pl.when(moves)
         def _():
             copy = fin_copy(key, out, out_rows, rows)
             copy.wait_send()
             copy.wait_recv()
+
+        @pl.when(helps)
+        def _():
+            pass_copy(key, out, out_rows, rows).wait_send()
 
         @pl.when(jnp.logical_not(moves))
         def _():
@@ -339,6 +400,9 @@
             pltpu.SemaphoreType.DMA((LEVELS, 2, 5)),
             pltpu.SemaphoreType.DMA((5,)),
             pltpu.SemaphoreType.DMA((5,)),
+            pltpu.VMEM((rows, order), F32),
+            pltpu.SemaphoreType.DMA((5,)),
+            pltpu.SemaphoreType.DMA((5,)),
         ],
         compiler_params=pltpu.CompilerParams(
             collective_id=0, has_side_effects=True, vmem_limit_bytes=60 * 1024 * 1024

time: 253 us -> 229 us (0.905)
  the two profiles are of different devices: /device:TPU:1 before, /device:TPU:2 now
where the time goes in v2:
time: 229 us
  Pallas kernels  224 us (98%)
  local copies, waits for them, and re-layouts  4.03 us (2%)
    pallas_call x1, Pallas kernels, per_device(): pl.pallas_call(functools.partial(kernel, n, order, columns, 2.5 ** 8 * ma...  224 us

profile of v2, /device:TPU:2, one launch (start us, length us, event | category | flops | bytes accessed | tf_op | source)
XLA Modules:
  0.0 228.8 jit_solution(15518272028624559938)
XLA Ops:
  0.6 224.1 %shard_map.58 = (f32[1,512,512]{2,1,0:T(8,128)}, f32[1,512,512]{2,1,0:T(8,128)}, f32[1,64,512]{2,1,0:T(8,128)}) custom-call(f32[1,512,512]{2,1,0:T(8,128)} %lower_ref.1, f32[1,512,512]{2,1,0:T(8,128)} %upper_ref.1, f32[1,64,512]{2,1,0:T(8,128)} %rhs_ref.1), custom_call_target="tpu_custom_call" | custom-call | tf_op jit(solution)/shard_map/pallas_call | solution.py:386
  224.7 0.0 copy-start
  224.7 2.4 %copy.9 = f32[1,512,512]{2,1,0:T(8,128)} copy(f32[1,512,512]{2,1,0:T(8,128)} %get-tuple-element.6) | data formatting | bytes 2097152
  227.1 0.0 copy-done
  227.1 0.0 copy-start.1
  227.1 1.0 copy.10
  228.1 0.1 copy-done.1
  228.1 0.7 copy.11
Async XLA Ops:
  224.7 2.4 %copy-start = (f32[1,512,512]{2,1,0:T(8,128)S(1)}, f32[1,512,512]{2,1,0:T(8,128)}, u32[]{:S(2)}) copy-start(f32[1,512,512]{2,1,0:T(8,128)} %get-tuple-element.7) | copy-start | bytes 3145732
  227.1 1.0 copy-start.1

commit v3 on v2

--- a/solution.py
+++ b/solution.py
@@ -248,33 +248,50 @@
                         send_held(level, piece - 1)
                 send_held(level, 4)
 
-        for piece in range(5):
+        def take_one(piece):
             wait_slot(1, piece, piece_rows(piece, 1 - f))
 
-        for which in range(2):
-            split_into(level, self_slot, which, sh, sl)
-            split_into(level, near_slot, which, nh, nl)
+        def staged(outer_pieces, inner_pieces):
+            @pl.when(outer)
+            def _():
+                for take, piece in outer_pieces:
+                    take(piece)
+
+            if inner is not None:
+                @pl.when(inner)
+                def _():
+                    for take, piece in inner_pieces:
+                        take(piece)
+
+        early = jnp.where(outer, f, 1 - f)
+        late = 1 - early
+        one_slot = jnp.where(outer, near_slot, 2)
+        two_slot = jnp.where(outer, 2, near_slot)
+
+        staged([(take_one, p) for p in range(5)], [(take_one, 0), (take_one, 1)])
+        split_into(level, self_slot, early, sh, sl)
+        split_into(level, one_slot, 0, nh, nl)
+        split_into(level, one_slot, 1, nh, nl)
 
         def add_term(r, value):
             term[block(r), :] = value
 
-        multiply(sh.at[f], sl.at[f], nh.at[1 - f], nl.at[1 - f], add_term)
-        multiply(sh.at[f], sl.at[f], nh.at[f], nl.at[f], store_split(xh.at[f], xl.at[f]))
-
-        @pl.when(outer)
-        def _():
-            for piece in range(5):
-                take_far(piece)
-
-        split_into(level, 2, 0, fh, fl)
-        split_into(level, 2, 1, fh, fl)
+        multiply(sh.at[early], sl.at[early], nh.at[late], nl.at[late], add_term)
+        multiply(sh.at[early], sl.at[early], nh.at[early], nl.at[early], store_split(xh.at[early], xl.at[early]))
+
+        staged([(take_far, 0), (take_far, 1)], [(take_one, 2), (take_one, 3)])
+        split_into(level, self_slot, late, sh, sl)
+        split_into(level, two_slot, late, fh, fl)
+        multiply(sh.at[late], sl.at[late], fh.at[late], fl.at[late], store_split(xh.at[late], xl.at[late]))
+        staged([(take_far, 2), (take_far, 3)], [])
+        split_into(level, two_slot, early, fh, fl)
 
         def finish_e(r, value):
             high, low = halves(term[block(r), :] + value)
             eh[block(r), :] = high
             el[block(r), :] = low
 
-        multiply(sh.at[1 - f], sl.at[1 - f], fh.at[f], fl.at[f], finish_e)
+        multiply(sh.at[late], sl.at[late], fh.at[early], fl.at[early], finish_e)
         multiply(eh, el, eh, el, store_split(qh, ql))
 
         def finish_y(r, value):
@@ -312,21 +329,16 @@
             def _():
                 send_fin_to(out_lower, 2 + r, block(r), rows)
 
-        @pl.loop(0, 2)
+        @pl.loop(0, 4)
         def _(piece):
             emit(piece)
 
-        multiply(sh.at[1 - f], sl.at[1 - f], fh.at[1 - f], fl.at[1 - f], store_split(xh.at[1 - f], xl.at[1 - f]))
-
-        @pl.loop(2, 4)
-        def _(piece):
-            emit(piece)
-
-        near_high, near_low = halves(bufs[level, near_slot, tail_rows(), :])
-        far_high, far_low = halves(bufs[level, 2, tail_rows(), :])
+        staged([(take_far, 4)], [(take_one, 4)])
+        near_high, near_low = halves(bufs[level, one_slot, tail_rows(), :])
+        far_high, far_low = halves(bufs[level, two_slot, tail_rows(), :])
         right = (bufs[level, self_slot, tail_rows(), :]
-                 - dot3(near_high, near_low, sh[f], sl[f], True)
-                 - dot3(far_high, far_low, sh[1 - f], sl[1 - f], True))
+                 - dot3(near_high, near_low, sh[early], sl[early], True)
+                 - dot3(far_high, far_low, sh[late], sl[late], True))
         right_high, right_low = halves(right)
         right = dot3(right_high, right_low, yh[...], yl[...], True)
         if level < LEVELS - 1:

time: 229 us -> 220 us (0.961)
  Pallas kernels: 224 us -> 215 us
    pallas_call x1, Pallas kernels: 224 us -> 215 us  [per_device(): pl.pallas_call(functools.partial(kernel, n, order, columns, 2.5 ** 8 * ma...]
where the time goes in v3:
time: 220 us
  Pallas kernels  215 us (98%)
  local copies, waits for them, and re-layouts  4.03 us (2%)
    pallas_call x1, Pallas kernels, per_device(): pl.pallas_call(functools.partial(kernel, n, order, columns, 2.5 ** 8 * ma...  215 us

profile of v3, /device:TPU:2, one launch (start us, length us, event | category | flops | bytes accessed | tf_op | source)
XLA Modules:
  0.0 219.6 jit_solution(4562078448886419670)
XLA Ops:
  0.6 214.9 %shard_map.58 = (f32[1,512,512]{2,1,0:T(8,128)}, f32[1,512,512]{2,1,0:T(8,128)}, f32[1,64,512]{2,1,0:T(8,128)}) custom-call(f32[1,512,512]{2,1,0:T(8,128)} %lower_ref.1, f32[1,512,512]{2,1,0:T(8,128)} %upper_ref.1, f32[1,64,512]{2,1,0:T(8,128)} %rhs_ref.1), custom_call_target="tpu_custom_call" | custom-call | tf_op jit(solution)/shard_map/pallas_call | solution.py:398
  215.5 0.0 copy-start
  215.5 2.4 %copy.9 = f32[1,512,512]{2,1,0:T(8,128)} copy(f32[1,512,512]{2,1,0:T(8,128)} %get-tuple-element.6) | data formatting | bytes 2097152
  217.9 0.0 copy-done
  217.9 0.0 copy-start.1
  217.9 1.0 copy.10
  218.9 0.1 copy-done.1
  218.9 0.7 copy.11
Async XLA Ops:
  215.5 2.4 %copy-start = (f32[1,512,512]{2,1,0:T(8,128)S(1)}, f32[1,512,512]{2,1,0:T(8,128)}, u32[]{:S(2)}) copy-start(f32[1,512,512]{2,1,0:T(8,128)} %get-tuple-element.7) | copy-start | bytes 3145732
  217.9 1.0 copy-start.1
